TPU v7x, 128 devices: a whole 4x4x4 slice. The times are simulated.
128 devices in a mesh: dp: 16 (over x_lo, z, core), chan: 8 (over y, x_hi).
Axes of the slice: x: 4 (x_hi: 2, x_lo: 2; x = x_hi * 2 + x_lo), y: 4, z: 4, core: 2. Of those that a mesh axis runs over, the one named last changes fastest.
Arguments:
- volume: bfloat16 [16, 512, 1024], P('dp', 'chan'), may hold values from -16 to 16
- w_first: bfloat16 [27, 512, 512], P(None, 'chan'), may hold values from -0.0546875 to 0.0546875
- gain: float32 [512], replicated, may hold values from 0.1 to 1.9
- w_second: bfloat16 [27, 512, 512], P(None, None, 'chan'), may hold values from -0.0546875 to 0.0546875
- cotangent: bfloat16 [16, 512, 1024], P('dp', 'chan'), may hold values from -8 to 8
Outputs:
- output: bfloat16 [16, 512, 1024], P('dp', 'chan')
- grad_volume: bfloat16 [16, 512, 1024], P('dp', 'chan')
- grad_w_first: float32 [27, 512, 512], P(None, 'chan')
- grad_gain: float32 [512], P('chan')
- grad_w_second: float32 [27, 512, 512], P(None, None, 'chan')
All inputs are finite; a program needn't handle non-finite values.
Results may differ from a plain program's by a relative error of at most 0.005.
Values may be sent and summed in bfloat16 or wider, within the bound.
A program may use at most 64 MiB of HBM per device.

v0:
```python
import math
import jax
import jax.numpy as jnp
from jax import lax
from jax.sharding import PartitionSpec as P

DEPTH = 4
HEIGHT = 16
WIDTH = 16
TAP_OFFSETS = [
    (plane_off, row_off, col_off)
    for plane_off in (-1, 0, 1)
    for row_off in (-1, 0, 1)
    for col_off in (-1, 0, 1)
]
NORM_EPS = 1e-05


def moved_cells(field, plane_off, row_off, col_off):
    cell_count = field.shape[1]
    plane_cells = HEIGHT * WIDTH
    offset = plane_off * plane_cells + row_off * WIDTH + col_off
    margin = plane_cells + WIDTH + 1
    padded = jnp.pad(field, ((0, 0), (margin, margin)))
    sliced = lax.slice_in_dim(padded, margin + offset, margin + offset + cell_count, axis=1)
    cells = jnp.arange(cell_count, dtype=jnp.int32)
    depth_at = cells // plane_cells + plane_off
    row_at = cells // WIDTH % HEIGHT + row_off
    col_at = cells % WIDTH + col_off
    inside = (
        (depth_at >= 0)
        & (depth_at < DEPTH)
        & (row_at >= 0)
        & (row_at < HEIGHT)
        & (col_at >= 0)
        & (col_at < WIDTH)
    )
    return jnp.where(inside[None, :], sliced, jnp.zeros_like(sliced))


def stack_taps(field, sign):
    layers = [
        moved_cells(field, sign * offsets[0], sign * offsets[1], sign * offsets[2])
        for offsets in TAP_OFFSETS
    ]
    return jnp.concatenate(layers, axis=0).reshape(27, field.shape[0], field.shape[1])


def block_rows(count):
    chosen = 1
    for trial in range(1, 65):
        if count % trial == 0:
            chosen = trial
    return chosen


def normalize(pre, gain_rows):
    center = pre - jnp.mean(pre, axis=1, keepdims=True)
    inverse = lax.rsqrt(jnp.mean(center * center, axis=1, keepdims=True) + NORM_EPS)
    normed = center * inverse
    scaled = gain_rows[:, None] * normed
    return (normed, inverse, scaled, jax.nn.silu(scaled).astype(jnp.bfloat16))


def normalize_back(dact, normed, inverse, scaled, gain_rows):
    sigma = jax.nn.sigmoid(scaled)
    dscaled = dact * sigma * (1.0 + scaled * (1.0 - sigma))
    gain_part = jnp.sum(dscaled * normed, axis=1)
    dnormed = dscaled * gain_rows[:, None]
    dpre = (
        dnormed
        - jnp.mean(dnormed, axis=1, keepdims=True)
        - normed * jnp.mean(dnormed * normed, axis=1, keepdims=True)
    ) * inverse
    return (gain_part, dpre.astype(jnp.bfloat16))


def shards(volume, w_first, gain, w_second, cotangent):
    local_rows = volume.shape[1]
    channels_all = w_first.shape[2]
    cell_count = volume.shape[2]
    source = volume[0]
    target = cotangent[0]
    chan_index = lax.axis_index("chan")
    volume_cols = stack_taps(source, 1)
    target_cols = stack_taps(target, -1)
    contract_first = (((0, 1), (0, 1)), ((), ()))
    contract_second = (((0, 2), (0, 1)), ((), ()))
    contract_cells = (((2,), (1,)), ((), ()))
    second_init = (
        jnp.zeros((local_rows, cell_count), jnp.float32),
        jnp.zeros((27, channels_all, local_rows), jnp.float32),
    )
    first_init = (
        jnp.zeros((local_rows, cell_count), jnp.float32),
        jnp.zeros((27, local_rows, channels_all), jnp.float32),
    )
    own_gain = lax.dynamic_slice_in_dim(gain, chan_index * local_rows, local_rows, 0)
    weights = w_first
    pre_own = lax.psum_scatter(
        lax.dot_general(weights, volume_cols, contract_first, preferred_element_type=jnp.float32),
        "chan",
        scatter_dimension=0,
        tiled=True,
    )
    normed, inverse, scaled, act_own = normalize(pre_own, own_gain)
    act_rows = lax.all_gather(act_own, "chan", axis=0, tiled=True)
    count = act_rows.shape[0]
    step_rows = block_rows(count)

    def second_one_block(index, inner):
        out_now, grad_now = inner
        begin = index * step_rows
        rows = lax.dynamic_slice_in_dim(act_rows, begin, step_rows, 0)
        cols = stack_taps(rows, 1)
        weights = lax.dynamic_slice_in_dim(w_second, begin, step_rows, 1)
        out_now = out_now + lax.dot_general(
            weights, cols, contract_first, preferred_element_type=jnp.float32
        )
        grad_part = lax.dot_general(
            cols, target, contract_cells, preferred_element_type=jnp.float32
        )
        grad_now = lax.dynamic_update_slice_in_dim(grad_now, grad_part, begin, 1)
        return (out_now, grad_now)

    out_sum, second_grad = lax.fori_loop(0, count // step_rows, second_one_block, second_init)
    output = out_sum.astype(jnp.bfloat16)[None]
    factor = 1.0 / math.sqrt(lax.axis_size("dp") * cell_count)
    weights = w_second
    dact_own = lax.psum_scatter(
        lax.dot_general(weights, target_cols, contract_second, preferred_element_type=jnp.float32),
        "chan",
        scatter_dimension=0,
        tiled=True,
    )
    gain_part, dpre_own = normalize_back(dact_own, normed, inverse, scaled, own_gain)
    grad_rows = lax.all_gather(dpre_own, "chan", axis=0, tiled=True)
    count = grad_rows.shape[0]
    first_step_rows = block_rows(count)

    def first_one_block(index, inner):
        back_now, grad_now = inner
        begin = index * first_step_rows
        rows = lax.dynamic_slice_in_dim(grad_rows, begin, first_step_rows, 0)
        cols = stack_taps(rows, -1)
        weights = lax.dynamic_slice_in_dim(w_first, begin, first_step_rows, 2)
        back_now = back_now + lax.dot_general(
            weights, cols, contract_second, preferred_element_type=jnp.float32
        )
        grad_part = lax.dot_general(
            volume_cols, rows, contract_cells, preferred_element_type=jnp.float32
        )
        grad_now = lax.dynamic_update_slice_in_dim(grad_now, grad_part, begin, 2)
        return (back_now, grad_now)

    back_sum, first_grad = lax.fori_loop(0, count // first_step_rows, first_one_block, first_init)
    first_total, second_total, gain_total = lax.psum((first_grad, second_grad, gain_part), "dp")
    grad_volume = back_sum.astype(jnp.bfloat16)[None]
    return (output, grad_volume, first_total * factor, gain_total * factor, second_total * factor)


def solution(mesh):
    placed = (
        P("dp", "chan", None),
        P(None, "chan", None),
        P(),
        P(None, None, "chan"),
        P("dp", "chan", None),
    )
    return jax.shard_map(
        shards,
        mesh=mesh,
        in_specs=placed,
        out_specs=(
            P("dp", "chan", None),
            P("dp", "chan", None),
            P(None, "chan", None),
            P("chan"),
            P(None, None, "chan"),
        ),
        check_vma=False,
    )
```

profile of v0, /device:TPU:0, one launch (start us, length us, event | category | flops | bytes accessed | tf_op | source)
XLA Modules:
  0.0 805.6 jit_solution(12205179865725809057)
XLA Ops:
  26.4 3.4 convolution_bitcast_fusion.4
  29.9 2.9 copy.16
  32.9 6.0 convolution_bitcast_fusion.3
  38.8 2.9 copy.18
  42.5 67.8 %reduce-scatter.7.cloned.1.call-done = f32[64,1024]{1,0:T(8,128)} async-done(((f32[512,1024]{1,0:T(8,128)}), f32[64,1024]{1,0:T(8,128)}) %reduce-scatter.7.cloned.1.call-update) | async-done | bytes 262160 | tf_op jit(solution)/shard_map/reduce_scatter | solution.py:100
  112.6 75.8 %reduce-scatter.9.cloned.1.call-done = f32[64,1024]{1,0:T(8,128)} async-done(((f32[512,1024]{1,0:T(8,128)}), f32[64,1024]{1,0:T(8,128)}) %reduce-scatter.9.cloned.1.call-update) | async-done | bytes 262160 | tf_op jit(solution)/shard_map/reduce_scatter | solution.py:130
  192.5 44.4 %all-gather.5.cloned.1.call-done = bf16[512,1024]{1,0:T(8,128)(2,1)} async-done(((bf16[64,1024]{1,0:T(8,128)(2,1)}), bf16[512,1024]{1,0:T(8,128)(2,1)}) %all-gather.5.cloned.1.call-update) | async-done | bytes 1048592 | tf_op jit(solution)/shard_map/all_gather | solution.py:137
  239.2 272.8 %while.39 = (s32[]{:T(128)}, f32[64,1024]{1,0:T(8,128)S(1)}, f32[27,64,512]{2,1,0:T(8,128)}, bf16[27,64,512]{2,1,0:T(8,128)(2,1)S(1)}, bf16[512,1024]{1,0:T(8,12...) while((s32[]{:T(128)}, f32[64,1024]{1,0:T(8,128)S(1)}, ...), condition=%wide.region_9.10_spmd.clone, body=%wide.region_8.9_spmd.clone.sunk | while | flops 456046592 | bytes 31054024 | solution.py:156
  261.5 3.1 fusion.437
  265.7 5.8 dynamic_update_slice.27
  293.9 3.1 fusion.437
  298.1 9.6 %dynamic_update_slice.27 = f32[27,64,512]{2,1,0:T(8,128)} dynamic-update-slice(f32[27,64,512]{2,1,0:T(8,128)} %get-tuple-element.591, f32[27,64,64]{2,1,0:T(8,128)S(1)} %convolution_bitcast_fusion.6, s32[]{:T(128)} %constant.1758.clone.1..sunk.1, s32[]{:T(128)} %constant.1758.clone.1..sunk.1, s32[]{:T(128)S(6)} %select_n.6693) | dynamic-update-slice | bytes 884740 | tf_op jit(solution)/shard_map/while/body/eval_jaxpr/dynamic_update_slice | solution.py:153
  330.1 3.1 fusion.437
  334.3 5.8 dynamic_update_slice.27
  362.5 3.1 fusion.437
  366.7 9.6 %dynamic_update_slice.27 = f32[27,64,512]{2,1,0:T(8,128)} dynamic-update-slice(f32[27,64,512]{2,1,0:T(8,128)} %get-tuple-element.591, f32[27,64,64]{2,1,0:T(8,128)S(1)} %convolution_bitcast_fusion.6, s32[]{:T(128)} %constant.1758.clone.1..sunk.1, s32[]{:T(128)} %constant.1758.clone.1..sunk.1, s32[]{:T(128)S(6)} %select_n.6693) | dynamic-update-slice | bytes 884740 | tf_op jit(solution)/shard_map/while/body/eval_jaxpr/dynamic_update_slice | solution.py:153
  398.6 3.1 fusion.437
  402.8 5.8 dynamic_update_slice.27
  431.0 3.1 fusion.437
  435.2 9.6 %dynamic_update_slice.27 = f32[27,64,512]{2,1,0:T(8,128)} dynamic-update-slice(f32[27,64,512]{2,1,0:T(8,128)} %get-tuple-element.591, f32[27,64,64]{2,1,0:T(8,128)S(1)} %convolution_bitcast_fusion.6, s32[]{:T(128)} %constant.1758.clone.1..sunk.1, s32[]{:T(128)} %constant.1758.clone.1..sunk.1, s32[]{:T(128)S(6)} %select_n.6693) | dynamic-update-slice | bytes 884740 | tf_op jit(solution)/shard_map/while/body/eval_jaxpr/dynamic_update_slice | solution.py:153
  467.2 3.1 fusion.437
  471.4 5.2 dynamic_update_slice.27
  499.0 3.1 fusion.437
  503.2 8.8 %dynamic_update_slice.27 = f32[27,64,512]{2,1,0:T(8,128)} dynamic-update-slice(f32[27,64,512]{2,1,0:T(8,128)} %get-tuple-element.591, f32[27,64,64]{2,1,0:T(8,128)S(1)} %convolution_bitcast_fusion.6, s32[]{:T(128)} %constant.1758.clone.1..sunk.1, s32[]{:T(128)} %constant.1758.clone.1..sunk.1, s32[]{:T(128)S(6)} %select_n.6693) | dynamic-update-slice | bytes 884740 | tf_op jit(solution)/shard_map/while/body/eval_jaxpr/dynamic_update_slice | solution.py:153
  514.3 139.8 %while.38 = (s32[]{:T(128)}, f32[64,1024]{1,0:T(8,128)}, f32[27,512,64]{1,2,0:T(8,128)}, bf16[27,512,64]{1,2,0:T(8,128)(2,1)}, bf16[512,1024]{1,0:T(8,128)(2,1)}...) while((s32[]{:T(128)}, f32[64,1024]{1,0:T(8,128)}, ...), condition=%wide.region_4.5_spmd.clone, body=%wide.region_3.4_spmd.clone.sunk | while | flops 456046592 | bytes 17422536 | solution.py:126
  519.2 2.7 fusion.406
  521.9 6.1 dynamic_update_slice.26
  535.6 2.7 fusion.406
  538.3 8.5 %dynamic_update_slice.26 = f32[27,512,64]{1,2,0:T(8,128)} dynamic-update-slice(f32[27,512,64]{1,2,0:T(8,128)} %get-tuple-element.561, f32[27,64,64]{1,2,0:T(8,128)} %fusion.406, s32[]{:T(128)} %constant.1758.clone.1..sunk, s32[]{:T(128)S(6)} %select_n.6557, s32[]{:T(128)} %constant.1758.clone.1..sunk) | dynamic-update-slice | bytes 884740 | tf_op jit(solution)/shard_map/while/body/eval_jaxpr/dynamic_update_slice | solution.py:123
  546.8 2.7 fusion.405
  557.2 6.1 dynamic_update_slice.26
  563.2 2.7 fusion.405
  573.6 8.5 %dynamic_update_slice.26 = f32[27,512,64]{1,2,0:T(8,128)} dynamic-update-slice(f32[27,512,64]{1,2,0:T(8,128)} %get-tuple-element.561, f32[27,64,64]{1,2,0:T(8,128)} %fusion.406, s32[]{:T(128)} %constant.1758.clone.1..sunk, s32[]{:T(128)S(6)} %select_n.6557, s32[]{:T(128)} %constant.1758.clone.1..sunk) | dynamic-update-slice | bytes 884740 | tf_op jit(solution)/shard_map/while/body/eval_jaxpr/dynamic_update_slice | solution.py:123
  582.1 2.7 fusion.405
  589.8 2.7 fusion.406
  592.5 6.1 dynamic_update_slice.26
  598.6 2.7 fusion.405
  606.2 2.7 fusion.406
  608.9 8.5 %dynamic_update_slice.26 = f32[27,512,64]{1,2,0:T(8,128)} dynamic-update-slice(f32[27,512,64]{1,2,0:T(8,128)} %get-tuple-element.561, f32[27,64,64]{1,2,0:T(8,128)} %fusion.406, s32[]{:T(128)} %constant.1758.clone.1..sunk, s32[]{:T(128)S(6)} %select_n.6557, s32[]{:T(128)} %constant.1758.clone.1..sunk) | dynamic-update-slice | bytes 884740 | tf_op jit(solution)/shard_map/while/body/eval_jaxpr/dynamic_update_slice | solution.py:123
  617.5 2.7 fusion.405
  627.8 5.4 dynamic_update_slice.26
  633.2 2.7 fusion.405
  640.9 2.7 fusion.406
  643.6 7.7 dynamic_update_slice.26
  651.3 2.7 fusion.405
  654.1 28.4 %psum.22 = f32[64]{0:T(128)S(1)} all-reduce(f32[64]{0:T(128)S(1)} %get-tuple-element.439), channel_id=1, replica_groups=mesh['dp'=16,'chan'=8] {'dp'}, use_global_device_ids=true, to_apply=%region_12.13 | all-reduce | flops 64 | bytes 512 | tf_op jit(solution)/shard_map/psum | solution.py:157
  684.4 107.9 %all-reduce.7.cloned.1.call-done = (f32[27,64,512]{2,1,0:T(8,128)}, f32[27,512,64]{1,2,0:T(8,128)}) async-done(((f32[27,64,512]{2,1,0:T(8,128)}, f32[27,512,64]{1,2,0:T(8,128)}), (f32[27,64,512]{2,1,0:T(8,128)}, f32[27,512,64]{1,2,0:T(8,128)})) %all-reduce.7.cloned.1.call-update) | async-done | bytes 7077904 | tf_op jit(solution)/shard_map/psum | solution.py:157
  792.3 4.6 broadcast_multiply_fusion
  (1049 shorter events, 269.2 us)
Async XLA Ops:
  7.2 13.5 %copy-start = (bf16[1,64,1024]{2,1,0:T(8,128)(2,1)S(1)}, bf16[1,64,1024]{2,1,0:T(8,128)(2,1)}, u32[]{:S(2)}) copy-start(bf16[1,64,1024]{2,1,0:T(8,128)(2,1)} %param.13) | copy-start | bytes 393220
  7.2 14.7 %copy-start.2 = (bf16[1,64,1024]{2,1,0:T(8,128)(2,1)S(1)}, bf16[1,64,1024]{2,1,0:T(8,128)(2,1)}, u32[]{:S(2)}) copy-start(bf16[1,64,1024]{2,1,0:T(8,128)(2,1)} %param.9) | copy-start | bytes 393220
  7.2 103.1 %reduce-scatter.7.cloned.1.call-start = ((), (), s32[]{:S(2)}) async-start(), calls=%async_computation.4 | async-start | bytes 2359296 | tf_op jit(solution)/shard_map/reduce_scatter | solution.py:100
  22.0 2.6 copy-start.10
  22.1 4.4 copy-start.9
  24.7 1.8 copy-start.3
  32.8 155.6 %reduce-scatter.9.cloned.1.call-start = ((), (), s32[]{:S(2)}) async-start(), calls=%async_computation.5 | async-start | bytes 2359296 | tf_op jit(solution)/shard_map/reduce_scatter | solution.py:130
  41.7 195.2 %all-gather.5.cloned.1.call-start = ((), (), s32[]{:S(2)}) async-start(), calls=%async_computation.3 | async-start | bytes 1179648 | tf_op jit(solution)/shard_map/all_gather | solution.py:137
  191.7 320.3 %all-gather.3.cloned.1.call-start = ((), (), s32[]{:S(2)}) async-start(), calls=%async_computation.2 | async-start | bytes 1179648 | tf_op jit(solution)/shard_map/all_gather | solution.py:107
  192.3 600.0 %all-reduce.7.cloned.1.call-start = ((), (), s32[]{:S(2)}) async-start(), calls=%async_computation.6 | async-start | bytes 14155776 | tf_op jit(solution)/shard_map/psum | solution.py:157
  261.5 3.1 copy-start.4
  293.9 3.1 copy-start.4
  330.1 3.1 copy-start.4
  362.5 3.1 copy-start.4
  398.6 3.1 copy-start.4
  431.0 3.1 copy-start.4
  467.2 3.1 copy-start.4
  499.0 3.1 copy-start.4
  512.0 2.2 copy-start.6
  515.2 4.0 copy-start.1
  531.6 4.0 copy-start.1
  550.5 4.0 copy-start.1
  566.9 4.0 copy-start.1
  585.8 4.0 copy-start.1
  602.2 4.0 copy-start.1
  621.1 4.0 copy-start.1
  636.9 4.0 copy-start.1
  654.0 29.0 %copy-start.7 = (f32[64,1024]{1,0:T(8,128)S(1)}, f32[64,1024]{1,0:T(8,128)}, u32[]{:S(2)}) copy-start(f32[64,1024]{1,0:T(8,128)} %copy-done.6) | copy-start | bytes 786436
  654.0 29.7 %copy-start.5 = (f32[64,1024]{1,0:T(8,128)S(1)}, f32[64,1024]{1,0:T(8,128)}, u32[]{:S(2)}) copy-start(f32[64,1024]{1,0:T(8,128)} %get-tuple-element.381) | copy-start | bytes 786436
  792.3 4.6 copy-start.8
Sparse Core Ops, SparseCore 0:
  32.9 77.3 reduce-scatter.6
  114.6 73.7 reduce-scatter.8
  191.8 45.0 all-gather.4
  239.7 45.0 all-gather.2
  654.2 138.0 all-reduce.6
where the time goes:
time: 809 us; the launch traced here: 806 us
  waiting for transfers between devices  297 us (37%)
  other arithmetic  232 us (29%)
  local copies, waits for them, and re-layouts  145 us (18%)
  matrix products  86.1 us (11%)
  blocking collectives  28.4 us (4%)
  between operations  14.4 us (2%)
    while x416, other arithmetic  189 us
    psum x1, waiting for transfers between devices, shards(): lax.psum((first_grad, second_grad, gain_part), 'dp')  108 us
    reduce_scatter x1, waiting for transfers between devices, shards(): lax.psum_scatter(lax.dot_general(weights, target_cols, contract_second, p...  75.8 us
    reduce_scatter x1, waiting for transfers between devices, shards(): lax.psum_scatter(lax.dot_general(weights, volume_cols, contract_first, pr...  67.8 us
    dynamic_update_slice x8, local copies, waits for them, and re-layouts, first_one_block(): grad_now = lax.dynamic_update_slice_in_dim(grad_now, grad_part, begin, 2)  60.5 us
    dynamic_update_slice x8, local copies, waits for them, and re-layouts, second_one_block(): grad_now = lax.dynamic_update_slice_in_dim(grad_now, grad_part, begin, 1)  56.9 us
    all_gather x1, waiting for transfers between devices, shards(): grad_rows = lax.all_gather(dpre_own, 'chan', axis=0, tiled=True)  44.4 us
    psum x1, blocking collectives, shards(): lax.psum((first_grad, second_grad, gain_part), 'dp')  28.4 us
  transfers between devices with their start and end apart: 5, of which 4 were waited for; matrix products, arithmetic and copies ran while one was open for 36% of the time, Pallas kernels for 0%

commit v1 on v0

--- a/solution.py
+++ b/solution.py
@@ -134,7 +134,9 @@
         tiled=True,
     )
     gain_part, dpre_own = normalize_back(dact_own, normed, inverse, scaled, own_gain)
-    grad_rows = lax.all_gather(dpre_own, "chan", axis=0, tiled=True)
+    grad_rows = jnp.concatenate(
+        lax.all_to_all(jnp.stack([dpre_own] * lax.axis_size("chan")), "chan", 0, 0), axis=0
+    )
     count = grad_rows.shape[0]
     first_step_rows = block_rows(count)
 

time: 809 us -> 770 us (0.952)
  waiting for transfers between devices: 297 us -> 267 us
    all_gather x1 -> x0, waiting for transfers between devices: 44.4 us -> none  [shards(): grad_rows = lax.all_gather(dpre_own, 'chan', axis=0, tiled=True)]
    all_to_all x0 -> x1, waiting for transfers between devices: none -> 14.9 us  [shards(): lax.all_to_all(jnp.stack([dpre_own] * lax.axis_size('chan')), 'chan', 0, 0)]
where the time goes in v1:
time: 770 us; the launch traced here: 766 us
  waiting for transfers between devices  267 us (35%)
  other arithmetic  225 us (29%)
  local copies, waits for them, and re-layouts  139 us (18%)
  matrix products  86.6 us (11%)
  blocking collectives  27.5 us (4%)
  between operations  14.4 us (2%)
    while x416, other arithmetic  182 us
    psum x1, waiting for transfers between devices, shards(): lax.psum((first_grad, second_grad, gain_part), 'dp')  107 us
    reduce_scatter x1, waiting for transfers between devices, shards(): lax.psum_scatter(lax.dot_general(weights, target_cols, contract_second, p...  75.8 us
    reduce_scatter x1, waiting for transfers between devices, shards(): lax.psum_scatter(lax.dot_general(weights, volume_cols, contract_first, pr...  68.4 us
    dynamic_update_slice x8, local copies, waits for them, and re-layouts, first_one_block(): grad_now = lax.dynamic_update_slice_in_dim(grad_now, grad_part, begin, 2)  60.5 us
    dynamic_update_slice x8, local copies, waits for them, and re-layouts, second_one_block(): grad_now = lax.dynamic_update_slice_in_dim(grad_now, grad_part, begin, 1)  56.9 us
    psum x1, blocking collectives, shards(): lax.psum((first_grad, second_grad, gain_part), 'dp')  27.5 us
    dot_general x8, matrix products, first_one_block(): lax.dot_general(weights, cols, contract_second, preferred_element_type=jn...  25.9 us
  transfers between devices with their start and end apart: 5, of which 4 were waited for; matrix products, arithmetic and copies ran while one was open for 36% of the time, Pallas kernels for 0%

profile of v1, /device:TPU:0, one launch (start us, length us, event | category | flops | bytes accessed | tf_op | source)
XLA Modules:
  0.0 766.4 jit_solution(3592475542503963388)
XLA Ops:
  26.4 3.4 convolution_bitcast_fusion.4
  29.8 3.1 copy.16
  33.0 5.4 convolution_bitcast_fusion.3
  38.4 2.9 copy.18
  42.1 68.4 %reduce-scatter.7.cloned.1.call-done = f32[64,1024]{1,0:T(8,128)} async-done(((f32[512,1024]{1,0:T(8,128)}), f32[64,1024]{1,0:T(8,128)}) %reduce-scatter.7.cloned.1.call-update) | async-done | bytes 262160 | tf_op jit(solution)/shard_map/reduce_scatter | solution.py:100
  112.7 75.8 %reduce-scatter.9.cloned.1.call-done = f32[64,1024]{1,0:T(8,128)} async-done(((f32[512,1024]{1,0:T(8,128)}), f32[64,1024]{1,0:T(8,128)}) %reduce-scatter.9.cloned.1.call-update) | async-done | bytes 262160 | tf_op jit(solution)/shard_map/reduce_scatter | solution.py:130
  192.9 3.9 all-to-all-start
  197.8 14.9 %all-to-all-done = bf16[8,64,1024]{2,1,0:T(8,128)(2,1)S(1)} async-done(((bf16[8,64,1024]{2,1,0:T(8,128)(2,1)}), bf16[8,64,1024]{2,1,0:T(8,128)(2,1)S(1)}, u32[]{:S(2)}, u32[]{:S(2)}) %all-to-all-start) | async-done | bytes 1048608 | tf_op jit(solution)/shard_map/all_to_all | solution.py:138
  215.0 259.6 %while.39 = (s32[]{:T(128)}, f32[64,1024]{1,0:T(8,128)S(1)}, f32[27,64,512]{2,1,0:T(8,128)}, bf16[27,64,512]{2,1,0:T(8,128)(2,1)}, bf16[512,1024]{1,0:T(8,128)(2...) while((s32[]{:T(128)}, f32[64,1024]{1,0:T(8,128)S(1)}, ...), condition=%wide.region_9.10_spmd.clone, body=%wide.region_8.9_spmd.clone.sunk | while | flops 456046592 | bytes 31054024 | solution.py:158
  235.5 3.2 fusion.437
  239.8 5.8 dynamic_update_slice.27
  266.2 3.2 fusion.437
  270.6 9.6 %dynamic_update_slice.27 = f32[27,64,512]{2,1,0:T(8,128)} dynamic-update-slice(f32[27,64,512]{2,1,0:T(8,128)} %get-tuple-element.585, f32[27,64,64]{2,1,0:T(8,128)S(1)} %convolution_bitcast_fusion.6, s32[]{:T(128)} %constant.1758.clone.1..sunk.1, s32[]{:T(128)} %constant.1758.clone.1..sunk.1, s32[]{:T(128)S(6)} %select_n.6693) | dynamic-update-slice | bytes 884740 | tf_op jit(solution)/shard_map/while/body/eval_jaxpr/dynamic_update_slice | solution.py:155
  300.8 3.2 fusion.437
  305.1 5.8 dynamic_update_slice.27
  331.5 3.2 fusion.437
  335.8 9.6 %dynamic_update_slice.27 = f32[27,64,512]{2,1,0:T(8,128)} dynamic-update-slice(f32[27,64,512]{2,1,0:T(8,128)} %get-tuple-element.585, f32[27,64,64]{2,1,0:T(8,128)S(1)} %convolution_bitcast_fusion.6, s32[]{:T(128)} %constant.1758.clone.1..sunk.1, s32[]{:T(128)} %constant.1758.clone.1..sunk.1, s32[]{:T(128)S(6)} %select_n.6693) | dynamic-update-slice | bytes 884740 | tf_op jit(solution)/shard_map/while/body/eval_jaxpr/dynamic_update_slice | solution.py:155
  366.0 3.2 fusion.437
  370.3 5.8 dynamic_update_slice.27
  396.7 3.2 fusion.437
  401.1 9.6 %dynamic_update_slice.27 = f32[27,64,512]{2,1,0:T(8,128)} dynamic-update-slice(f32[27,64,512]{2,1,0:T(8,128)} %get-tuple-element.585, f32[27,64,64]{2,1,0:T(8,128)S(1)} %convolution_bitcast_fusion.6, s32[]{:T(128)} %constant.1758.clone.1..sunk.1, s32[]{:T(128)} %constant.1758.clone.1..sunk.1, s32[]{:T(128)S(6)} %select_n.6693) | dynamic-update-slice | bytes 884740 | tf_op jit(solution)/shard_map/while/body/eval_jaxpr/dynamic_update_slice | solution.py:155
  431.2 3.2 fusion.437
  435.6 5.2 dynamic_update_slice.27
  461.4 3.2 fusion.437
  465.7 8.8 %dynamic_update_slice.27 = f32[27,64,512]{2,1,0:T(8,128)} dynamic-update-slice(f32[27,64,512]{2,1,0:T(8,128)} %get-tuple-element.585, f32[27,64,64]{2,1,0:T(8,128)S(1)} %convolution_bitcast_fusion.6, s32[]{:T(128)} %constant.1758.clone.1..sunk.1, s32[]{:T(128)} %constant.1758.clone.1..sunk.1, s32[]{:T(128)S(6)} %select_n.6693) | dynamic-update-slice | bytes 884740 | tf_op jit(solution)/shard_map/while/body/eval_jaxpr/dynamic_update_slice | solution.py:155
  476.8 139.6 %while.38 = (s32[]{:T(128)}, f32[64,1024]{1,0:T(8,128)}, f32[27,512,64]{1,2,0:T(8,128)}, bf16[27,512,64]{1,2,0:T(8,128)(2,1)}, bf16[512,1024]{1,0:T(8,128)(2,1)}...) while((s32[]{:T(128)}, f32[64,1024]{1,0:T(8,128)}, ...), condition=%wide.region_4.5_spmd.clone, body=%wide.region_3.4_spmd.clone.sunk | while | flops 456046592 | bytes 17422536 | solution.py:126
  484.4 6.1 dynamic_update_slice.26
  498.1 2.7 fusion.406
  500.8 8.5 %dynamic_update_slice.26 = f32[27,512,64]{1,2,0:T(8,128)} dynamic-update-slice(f32[27,512,64]{1,2,0:T(8,128)} %get-tuple-element.555, f32[27,64,64]{1,2,0:T(8,128)} %fusion.406, s32[]{:T(128)} %constant.1758.clone.1..sunk, s32[]{:T(128)S(6)} %select_n.6557, s32[]{:T(128)} %constant.1758.clone.1..sunk) | dynamic-update-slice | bytes 884740 | tf_op jit(solution)/shard_map/while/body/eval_jaxpr/dynamic_update_slice | solution.py:123
  509.3 2.7 fusion.405
  516.9 2.7 fusion.406
  519.6 6.1 dynamic_update_slice.26
  525.7 2.7 fusion.405
  533.4 2.7 fusion.406
  536.1 8.5 %dynamic_update_slice.26 = f32[27,512,64]{1,2,0:T(8,128)} dynamic-update-slice(f32[27,512,64]{1,2,0:T(8,128)} %get-tuple-element.555, f32[27,64,64]{1,2,0:T(8,128)} %fusion.406, s32[]{:T(128)} %constant.1758.clone.1..sunk, s32[]{:T(128)S(6)} %select_n.6557, s32[]{:T(128)} %constant.1758.clone.1..sunk) | dynamic-update-slice | bytes 884740 | tf_op jit(solution)/shard_map/while/body/eval_jaxpr/dynamic_update_slice | solution.py:123
  544.6 2.7 fusion.405
  554.9 6.1 dynamic_update_slice.26
  561.0 2.7 fusion.405
  568.7 2.7 fusion.406
  571.4 8.5 %dynamic_update_slice.26 = f32[27,512,64]{1,2,0:T(8,128)} dynamic-update-slice(f32[27,512,64]{1,2,0:T(8,128)} %get-tuple-element.555, f32[27,64,64]{1,2,0:T(8,128)} %fusion.406, s32[]{:T(128)} %constant.1758.clone.1..sunk, s32[]{:T(128)S(6)} %select_n.6557, s32[]{:T(128)} %constant.1758.clone.1..sunk) | dynamic-update-slice | bytes 884740 | tf_op jit(solution)/shard_map/while/body/eval_jaxpr/dynamic_update_slice | solution.py:123
  579.9 2.7 fusion.405
  590.2 5.4 dynamic_update_slice.26
  595.6 2.7 fusion.405
  606.0 7.7 %dynamic_update_slice.26 = f32[27,512,64]{1,2,0:T(8,128)} dynamic-update-slice(f32[27,512,64]{1,2,0:T(8,128)} %get-tuple-element.555, f32[27,64,64]{1,2,0:T(8,128)} %fusion.406, s32[]{:T(128)} %constant.1758.clone.1..sunk, s32[]{:T(128)S(6)} %select_n.6557, s32[]{:T(128)} %constant.1758.clone.1..sunk) | dynamic-update-slice | bytes 884740 | tf_op jit(solution)/shard_map/while/body/eval_jaxpr/dynamic_update_slice | solution.py:123
  613.7 2.7 fusion.405
  616.4 27.5 %psum.22 = f32[64]{0:T(128)S(1)} all-reduce(f32[64]{0:T(128)S(1)} %get-tuple-element.433), channel_id=1, replica_groups=mesh['dp'=16,'chan'=8] {'dp'}, use_global_device_ids=true, to_apply=%region_12.13 | all-reduce | flops 64 | bytes 512 | tf_op jit(solution)/shard_map/psum | solution.py:159
  645.8 107.2 %all-reduce.7.cloned.1.call-done = (f32[27,64,512]{2,1,0:T(8,128)}, f32[27,512,64]{1,2,0:T(8,128)}) async-done(((f32[27,64,512]{2,1,0:T(8,128)}, f32[27,512,64]{1,2,0:T(8,128)}), (f32[27,64,512]{2,1,0:T(8,128)}, f32[27,512,64]{1,2,0:T(8,128)})) %all-reduce.7.cloned.1.call-update) | async-done | bytes 7077904 | tf_op jit(solution)/shard_map/psum | solution.py:159
  753.1 4.6 broadcast_multiply_fusion
  (1051 shorter events, 258.7 us)
Async XLA Ops:
  7.2 13.5 %copy-start = (bf16[1,64,1024]{2,1,0:T(8,128)(2,1)S(1)}, bf16[1,64,1024]{2,1,0:T(8,128)(2,1)}, u32[]{:S(2)}) copy-start(bf16[1,64,1024]{2,1,0:T(8,128)(2,1)} %param.13) | copy-start | bytes 393220
  7.2 14.7 %copy-start.2 = (bf16[1,64,1024]{2,1,0:T(8,128)(2,1)S(1)}, bf16[1,64,1024]{2,1,0:T(8,128)(2,1)}, u32[]{:S(2)}) copy-start(bf16[1,64,1024]{2,1,0:T(8,128)(2,1)} %param.9) | copy-start | bytes 393220
  7.2 103.3 %reduce-scatter.7.cloned.1.call-start = ((), (), s32[]{:S(2)}) async-start(), calls=%async_computation.4 | async-start | bytes 2359296 | tf_op jit(solution)/shard_map/reduce_scatter | solution.py:100
  22.0 2.6 copy-start.11
  22.1 4.4 copy-start.9
  24.7 1.8 copy-start.3
  29.8 3.1 copy-start.10
  32.9 155.6 %reduce-scatter.9.cloned.1.call-start = ((), (), s32[]{:S(2)}) async-start(), calls=%async_computation.5 | async-start | bytes 2359296 | tf_op jit(solution)/shard_map/reduce_scatter | solution.py:130
  192.9 19.8 %all-to-all-start = ((bf16[8,64,1024]{2,1,0:T(8,128)(2,1)}), bf16[8,64,1024]{2,1,0:T(8,128)(2,1)S(1)}, u32[]{:S(2)}, u32[]{:S(2)}) async-start(bf16[8,64,1024]{2,1,0:T(8,128)(2,1)} %stack.2), calls=%async_computation | async-start | bytes 2097152 | tf_op jit(solution)/shard_map/all_to_all | solution.py:138
  196.8 277.7 %all-gather.2.cloned.1.call-start = ((), (), s32[]{:S(2)}) async-start(), calls=%async_computation.3 | async-start | bytes 1179648 | tf_op jit(solution)/shard_map/all_gather | solution.py:107
  197.6 555.5 %all-reduce.7.cloned.1.call-start = ((), (), s32[]{:S(2)}) async-start(), calls=%async_computation.6 | async-start | bytes 14155776 | tf_op jit(solution)/shard_map/psum | solution.py:159
  235.5 3.3 copy-start.4
  266.2 3.3 copy-start.4
  300.8 3.3 copy-start.4
  331.5 3.3 copy-start.4
  366.0 3.3 copy-start.4
  396.7 3.3 copy-start.4
  431.2 3.3 copy-start.4
  461.4 3.2 copy-start.4
  474.5 2.2 copy-start.6
  477.7 4.0 copy-start.1
  494.1 4.0 copy-start.1
  512.9 4.0 copy-start.1
  529.4 4.0 copy-start.1
  548.2 4.0 copy-start.1
  564.7 4.0 copy-start.1
  583.5 4.0 copy-start.1
  599.3 4.0 copy-start.1
  616.4 28.1 %copy-start.7 = (f32[64,1024]{1,0:T(8,128)S(1)}, f32[64,1024]{1,0:T(8,128)}, u32[]{:S(2)}) copy-start(f32[64,1024]{1,0:T(8,128)} %copy-done.6) | copy-start | bytes 786436
  616.4 28.8 %copy-start.5 = (f32[64,1024]{1,0:T(8,128)S(1)}, f32[64,1024]{1,0:T(8,128)}, u32[]{:S(2)}) copy-start(f32[64,1024]{1,0:T(8,128)} %get-tuple-element.381) | copy-start | bytes 786436
  753.1 4.6 copy-start.8
Sparse Core Ops, SparseCore 0:
  33.0 77.3 reduce-scatter.6
  114.7 73.7 reduce-scatter.8
  200.6 48.3 all-gather.1
  616.6 136.4 all-reduce.6
